TPU v7x, 512 devices: a whole 4x8x8 slice. The times are simulated.
512 devices in a mesh: dp: 8 (over y), row: 4 (over z_lo), col: 16 (over x, z_hi, core).
Axes of the slice: x: 4, y: 8, z: 8 (z_hi: 2, z_lo: 4; z = z_hi * 4 + z_lo), core: 2. Of those that a mesh axis runs over, the one named last changes fastest.
Arguments:
- tokens: bfloat16 [2048, 4096], P(('dp', 'col'), 'row'), may hold values from -6 to 6
- gate_weight: bfloat16 [4096, 14336], P('row', 'col'), may hold values from -0.125 to 0.125
- up_weight: bfloat16 [4096, 14336], P('row', 'col'), may hold values from -0.125 to 0.125
- gate_mask: int32 [32, 112], P('row', 'col'), may hold values 0 or 1
- up_mask: int32 [32, 112], P('row', 'col'), may hold values 0 or 1
- slope: bfloat16 [2048, 14336], P(('dp', 'row'), 'col'), may hold values from -6 to 6
Outputs:
- hidden: bfloat16 [2048, 14336], P(('dp', 'row'), 'col')
- input_grad: bfloat16 [2048, 4096], P(('dp', 'col'), 'row')
- gate_grad: bfloat16 [32, 128, 14336], P('row', 'dp', 'col')
- up_grad: bfloat16 [32, 128, 14336], P('row', 'dp', 'col')
Inputs may be any that keep to these rules, and one draw needn't show every extreme that they name: `gate_mask`: 1 marks a live 128 x 128 block of the projection, 0 a pruned one. `up_mask`: 1 marks a live 128 x 128 block of the projection, 0 a pruned one.
All inputs are finite; a program needn't handle non-finite values.
Results may differ from a plain program's by a relative error of at most 0.0058.
Values may be sent and summed in bfloat16 or wider, within the bound.
No kernel may reach another device: no remote copies, remote signals or barrier semaphores. Data moves between devices by JAX's collectives and lax.ppermute only.
A program may use at most 64 MiB of HBM per device.

v0:
```python
import jax
import jax.numpy as jnp
from jax import lax
from jax.sharding import PartitionSpec as P


def expand_mask(mask, block, height):
    blocks_down, blocks_across = mask.shape
    grid = mask.astype(jnp.float32)[:, None, :, None]
    return jnp.broadcast_to(grid, (blocks_down, height, blocks_across, block)).reshape(
        blocks_down, height, blocks_across * block
    )


def body(tokens, gate_weight, up_weight, gate_mask, up_mask, slope):
    block = gate_weight.shape[0] // gate_mask.shape[0]
    width_part = gate_weight.shape[0]
    hidden_part = gate_weight.shape[1]
    gate_live = (
        gate_weight.astype(jnp.float32)
        * expand_mask(gate_mask, block, block).reshape(width_part, hidden_part)
    ).astype(jnp.bfloat16)
    up_live = (
        up_weight.astype(jnp.float32)
        * expand_mask(up_mask, block, block).reshape(width_part, hidden_part)
    ).astype(jnp.bfloat16)
    paired = jnp.concatenate([gate_live, up_live], axis=1)
    gathered = lax.all_gather(tokens, "col", axis=0, tiled=True)
    replica_tokens = gathered.shape[0]
    rows_here = gathered
    sums = lax.psum_scatter(
        jnp.dot(rows_here, paired, preferred_element_type=jnp.float32),
        "row",
        scatter_dimension=0,
        tiled=True,
    )
    gate = sums[:, :hidden_part]
    up = sums[:, hidden_part:]
    sigma = jax.nn.sigmoid(gate)
    act = gate * sigma
    hidden = (act * up).astype(jnp.bfloat16)
    slope_wide = slope.astype(jnp.float32)
    gate_slope = (slope_wide * up * sigma * (1.0 + gate * (1.0 - sigma))).astype(jnp.bfloat16)
    up_slope = (slope_wide * act).astype(jnp.bfloat16)
    slopes = jnp.concatenate([gate_slope, up_slope], axis=1)
    replica = lax.axis_index("dp")
    replicas = lax.axis_size("dp")
    share = block // replicas
    blocks_down = width_part // block
    everyone = lax.all_gather(slopes, ("dp", "row"), axis=0, tiled=True)
    local_slopes = lax.dynamic_slice_in_dim(everyone, replica * replica_tokens, replica_tokens, 0)
    by_owner = gathered.reshape(replica_tokens, blocks_down, replicas, share)
    by_owner = jnp.transpose(by_owner, (2, 0, 1, 3)).reshape(
        replicas, replica_tokens, blocks_down * share
    )
    feats = lax.all_to_all(by_owner, "dp", split_axis=0, concat_axis=0, tiled=True)
    partial_value = jnp.einsum(
        "ptk,ptf->pkf",
        feats,
        everyone.reshape(replicas, replica_tokens, -1),
        preferred_element_type=jnp.float32,
    )
    rounded = lax.optimization_barrier(partial_value.astype(jnp.bfloat16))
    grads = jnp.sum(rounded.astype(jnp.float32), axis=0).reshape(
        blocks_down, share, 2 * hidden_part
    )
    rows_here = local_slopes
    input_grad = lax.psum_scatter(
        lax.dot_general(
            rows_here, paired, (((1,), (1,)), ((), ())), preferred_element_type=jnp.float32
        ),
        "col",
        scatter_dimension=0,
        tiled=True,
    ).astype(jnp.bfloat16)
    gate_grad = (grads[:, :, :hidden_part] * expand_mask(gate_mask, block, share)).astype(
        jnp.bfloat16
    )
    up_grad = (grads[:, :, hidden_part:] * expand_mask(up_mask, block, share)).astype(jnp.bfloat16)
    return (hidden, input_grad, gate_grad, up_grad)


def solution(mesh):
    return jax.shard_map(
        body,
        mesh=mesh,
        in_specs=(
            P(("dp", "col"), "row"),
            P("row", "col"),
            P("row", "col"),
            P("row", "col"),
            P("row", "col"),
            P(("dp", "row"), "col"),
        ),
        out_specs=(
            P(("dp", "row"), "col"),
            P(("dp", "col"), "row"),
            P("row", "dp", "col"),
            P("row", "dp", "col"),
        ),
        check_vma=False,
    )
```

profile of v0, /device:TPU:6, one launch (start us, length us, event | category | flops | bytes accessed | tf_op | source)
XLA Modules:
  0.0 386.4 jit_solution(408374661671901712)
XLA Ops:
  7.2 0.0 copy-start.5
  7.2 0.0 reduce-scatter.7.cloned.1.call-start
  7.2 36.8 %all_gather.6 = bf16[256,1024]{1,0:T(8,128)(2,1)S(1)} all-gather(bf16[16,1024]{1,0:T(8,128)(2,1)} %param.6), channel_id=1, replica_groups=mesh['dp'=8,'row'=4,'col'=16] {'col'}, dimensions={0}, use_global_device_ids=true | all-gather | bytes 557056 | tf_op jit(solution)/shard_map/all_gather | solution.py:28
  44.0 0.7 convert_element_type.54
  44.7 0.1 copy.45
  44.8 2.9 copy.44
  47.7 0.0 copy-done.5
  47.7 0.1 copy.43
  47.8 3.8 copy.42
  51.6 0.0 copy-start
  51.6 0.3 broadcast_in_dim.33
  51.9 0.3 broadcast_in_dim.32
  52.2 0.9 copy-done
  53.1 2.5 fusion
  55.6 0.0 copy-start.1
  55.6 0.0 copy-start.3
  55.6 1.2 copy-done.1
  56.8 0.6 copy-done.3
  57.4 1.2 convolution_bitcast_fusion
  58.6 0.0 copy-start.4
  58.7 1.7 copy.57
  60.4 0.0 reduce-scatter.7.cloned.1.call-update
  60.4 0.0 all-gather.2.cloned.1.call-start
  60.5 0.0 copy-done.4
  60.5 0.8 copy.46
  61.3 46.4 %reduce-scatter.7.cloned.1.call-done = f32[64,1792]{1,0:T(8,128)} async-done(((f32[256,1792]{1,0:T(8,128)}), f32[64,1792]{1,0:T(8,128)}) %reduce-scatter.7.cloned.1.call-update) | async-done | bytes 458768
  107.7 1.1 fusion.15
  108.8 0.2 copy.60
  109.0 0.2 copy.59
  109.2 0.0 copy-start.2
  109.2 1.4 fusion.7
  110.6 0.1 pad_maximum_fusion.3
  110.7 0.9 copy.47
  111.6 0.0 all-gather.2.cloned.1.call-update
  111.6 0.2 copy.48
  111.9 1.0 copy.50
  112.9 6.7 %all-to-all-start = ((bf16[8,256,128]{2,1,0:T(8,128)(2,1)}), bf16[8,256,128]{2,1,0:T(8,128)(2,1)S(1)}, u32[]{:S(2)}, u32[]{:S(2)}) async-start(bf16[8,256,128]{2,1,0:T(8,128)(2,1)} %copy.50), calls=%async_computation.1 | async-start | bytes 1048576 | tf_op jit(solution)/shard_map/all_to_all | solution.py:56
  119.6 0.0 reduce-scatter.5.cloned.1.call-start
  119.7 166.3 %all-gather.2.cloned.1.call-done = bf16[2048,1792]{1,0:T(8,128)(2,1)} async-done(((bf16[64,1792]{1,0:T(8,128)(2,1)}), bf16[2048,1792]{1,0:T(8,128)(2,1)}) %all-gather.2.cloned.1.call-update) | async-done | bytes 7340048 | tf_op jit(solution)/shard_map/all_gather | solution.py:50
  285.9 0.0 copy-done.2
  285.9 3.9 %fusion.3 = f32[256,1024]{1,0:T(8,128)} fusion(bf16[1024,896]{0,1:T(8,128)(2,1)S(1)} %copy-done.2, bf16[1024,896]{0,1:T(8,128)(2,1)} %copy-done.3, bf16[2048,1792]{1,0:T(8,128)(2,1)} %all-gather.2.cloned.1.call-done, s32[]{:T(128)S(6)} %select_n.3), kind=kOutput, calls=%fused_computation.9 | convolution fusion | flops 946864128 | bytes 5636100 | tf_op jit(solution)/shard_map/dot_general | solution.py:69
  289.8 0.0 reduce-scatter.5.cloned.1.call-update
  289.8 0.1 broadcast_bitcast_fusion
  289.9 0.8 copy.55
  290.7 0.0 all-to-all-done
  290.7 5.5 %fusion.2 = bf16[8,128,1792]{1,2,0:T(8,128)(2,1)S(1)} fusion(bf16[8,256,1792]{2,1,0:T(8,128)(2,1)} %bitcast.36, bf16[8,256,128]{2,1,0:T(8,128)(2,1)S(1)} %all-to-all-done), kind=kOutput, calls=%fused_computation.7 | convolution fusion | flops 941359104 | bytes 11534336 | tf_op jit(solution)/shard_map/ptk,ptf->pkf/dot_general | solution.py:57
  296.2 0.5 convert_reduce_fusion
  296.8 0.3 copy.52
  297.1 0.8 fusion.9
  297.9 80.5 %reduce-scatter.5.cloned.1.call-done = f32[16,1024]{1,0:T(8,128)} async-done(((f32[256,1024]{1,0:T(8,128)}), f32[16,1024]{1,0:T(8,128)}) %reduce-scatter.5.cloned.1.call-update) | async-done | bytes 65552 | tf_op jit(solution)/shard_map/reduce_scatter | solution.py:68
  378.4 1.5 convert_element_type.60
  (2 shorter events, 0.0 us)
Async XLA Ops:
  7.2 40.5 %copy-start.5 = (s32[8,7]{1,0:T(8,128)S(1)}, s32[8,7]{1,0:T(8,128)}, u32[]{:S(2)}) copy-start(s32[8,7]{1,0:T(8,128)} %param.9) | copy-start | bytes 676
  7.2 100.6 %reduce-scatter.7.cloned.1.call-start = ((), (), s32[]{:S(2)}) async-start(), calls=%async_computation.5 | async-start | bytes 2293760
  51.6 1.5 copy-start
  55.6 1.2 copy-start.1
  55.6 1.8 copy-start.3
  58.6 1.8 copy-start.4
  60.4 225.5 %all-gather.2.cloned.1.call-start = ((), (), s32[]{:S(2)}) async-start(), calls=%async_computation.3 | async-start | bytes 7569408 | tf_op jit(solution)/shard_map/all_gather | solution.py:50
  109.2 176.7 %copy-start.2 = (bf16[1024,896]{0,1:T(8,128)(2,1)S(1)}, bf16[1024,896]{0,1:T(8,128)(2,1)}, u32[]{:S(2)}) copy-start(bf16[1024,896]{0,1:T(8,128)(2,1)} %copy-done.1) | copy-start | bytes 5505028
  112.9 177.8 %all-to-all-start = ((bf16[8,256,128]{2,1,0:T(8,128)(2,1)}), bf16[8,256,128]{2,1,0:T(8,128)(2,1)S(1)}, u32[]{:S(2)}, u32[]{:S(2)}) async-start(bf16[8,256,128]{2,1,0:T(8,128)(2,1)} %copy.50), calls=%async_computation.1 | async-start | bytes 1048576 | tf_op jit(solution)/shard_map/all_to_all | solution.py:56
  119.6 258.8 %reduce-scatter.5.cloned.1.call-start = ((), (), s32[]{:S(2)}) async-start(), calls=%async_computation.4 | async-start | bytes 1114112 | tf_op jit(solution)/shard_map/reduce_scatter | solution.py:68
Sparse Core Ops, SparseCore 0:
  60.5 47.1 reduce-scatter.6
  111.7 174.1 all-gather.1
  290.6 87.6 reduce-scatter.4
where the time goes:
time: 387 us; the launch traced here: 386 us
  waiting for transfers between devices  293 us (76%)
  blocking collectives  36.8 us (10%)
  local copies, waits for them, and re-layouts  17.5 us (5%)
  between operations  13.9 us (4%)
  matrix products  10.6 us (3%)
  other arithmetic  7.47 us (2%)
  starting transfers between devices  6.86 us (2%)
    all_gather x1, waiting for transfers between devices, body(): everyone = lax.all_gather(slopes, ('dp', 'row'), axis=0, tiled=True)  166 us
    reduce_scatter x1, waiting for transfers between devices, body(): lax.psum_scatter(lax.dot_general(rows_here, paired, (((1,), (1,)), ((), (...  80.5 us
    unnamed x4, waiting for transfers between devices  46.5 us
    all_gather x1, blocking collectives, body(): gathered = lax.all_gather(tokens, 'col', axis=0, tiled=True)  36.8 us
    unnamed x19, local copies, waits for them, and re-layouts  13.2 us
  transfers between devices with their start and end apart: 4, of which 3 were waited for; matrix products, arithmetic and copies ran while one was open for 4% of the time, Pallas kernels for 0%

commit v1 on v0

v1 whole, which is shorter than its diff:
```python
import jax
import jax.numpy as jnp
from jax import lax
from jax.experimental import pallas as pl
from jax.experimental.pallas import tpu as pltpu
from jax.sharding import PartitionSpec as P

BF = jnp.bfloat16
F32 = jnp.float32
FIRST_SHARE = 4


def masked_pair(gate_w, up_w, gate_mask, up_mask, block, column):
    rows = gate_w.shape[0] // block
    pieces = []
    for b in range(rows):
        part = pl.ds(b * block, block)
        g = gate_w[part, :].astype(F32) * gate_mask[b, column].astype(F32)
        u = up_w[part, :].astype(F32) * up_mask[b, column].astype(F32)
        pieces.append(jnp.concatenate([g, u], axis=1).astype(BF))
    return jnp.concatenate(pieces, axis=0)


def forward(tokens, gate_weight, up_weight, gate_mask, up_mask, first, count):
    block = gate_weight.shape[0] // gate_mask.shape[0]
    toks, depth = tokens.shape

    def kernel(gm, um, t, gw, uw, out):
        pair = masked_pair(gw, uw, gm, um, block, pl.program_id(0) + first)
        out[...] = jnp.dot(t[...], pair, preferred_element_type=F32).astype(BF)

    smem = pl.BlockSpec(memory_space=pltpu.SMEM)
    return pl.pallas_call(
        kernel,
        grid=(count,),
        in_specs=[
            smem,
            smem,
            pl.BlockSpec((toks, depth), lambda j: (0, 0)),
            pl.BlockSpec((depth, block), lambda j: (0, j + first)),
            pl.BlockSpec((depth, block), lambda j: (0, j + first)),
        ],
        out_specs=pl.BlockSpec((toks, 2 * block), lambda j: (0, j)),
        out_shape=jax.ShapeDtypeStruct((toks, count * 2 * block), BF),
        cost_estimate=pl.CostEstimate(
            flops=4 * toks * depth * count * block,
            bytes_accessed=4 * depth * count * block + 2 * toks * depth,
            transcendentals=0,
        ),
        name="forward",
    )(gate_mask, up_mask, tokens, gate_weight, up_weight)


def activate(received, slope, block, first, count, replicas_of_sum, hidden_before):
    here = slope.shape[0]

    def kernel(*refs):
        r, s = refs[0], refs[1]
        hidden, slopes = refs[-2], refs[-1]
        total = r[pl.ds(0, here), :].astype(F32)
        for k in range(1, replicas_of_sum):
            total = total + r[pl.ds(k * here, here), :].astype(F32)
        gate, up = total[:, :block], total[:, block:]
        sigma = jax.nn.sigmoid(gate)
        act = gate * sigma
        hidden[...] = (act * up).astype(BF)
        wide = s[...].astype(F32)
        gate_slope = (wide * up * sigma * (1.0 + gate * (1.0 - sigma))).astype(BF)
        slopes[...] = jnp.concatenate([gate_slope, (wide * act).astype(BF)], axis=1)

    in_specs = [
        pl.BlockSpec((here * replicas_of_sum, 2 * block), lambda j: (0, j)),
        pl.BlockSpec((here, block), lambda j: (0, j + first)),
    ]
    operands = [received, slope]
    aliases = {}
    if hidden_before is not None:
        in_specs.append(pl.BlockSpec(memory_space=pl.ANY))
        operands.append(hidden_before)
        aliases = {2: 0}
    return pl.pallas_call(
        kernel,
        grid=(count,),
        in_specs=in_specs,
        out_specs=[
            pl.BlockSpec((here, block), lambda j: (0, j + first)),
            pl.BlockSpec((here, 2 * block), lambda j: (0, j)),
        ],
        out_shape=[
            jax.ShapeDtypeStruct(slope.shape, BF),
            jax.ShapeDtypeStruct((here, count * 2 * block), BF),
        ],
        input_output_aliases=aliases,
        cost_estimate=pl.CostEstimate(
            flops=30 * here * count * block,
            bytes_accessed=here * count * block * 24,
            transcendentals=here * count * block,
        ),
        name="activate",
    )(*operands)


def parts_of(tokens, slopes, block, replicas, count):
    toks, depth = tokens.shape
    share = block // replicas
    blocks_down = depth // block

    def kernel(t, s, out, flipped):
        @pl.when(pl.program_id(0) == 0)
        def _():
            turned = t[...].T
            for b in range(blocks_down):
                for d in range(replicas):
                    flipped[pl.ds((d * blocks_down + b) * share, share), :] = turned[
                        b * block + d * share : b * block + (d + 1) * share, :
                    ]

        out[...] = jnp.dot(flipped[...], s[...], preferred_element_type=F32).astype(BF)

    return pl.pallas_call(
        kernel,
        grid=(count,),
        in_specs=[
            pl.BlockSpec((toks, depth), lambda j: (0, 0)),
            pl.BlockSpec((toks, 2 * block), lambda j: (0, j)),
        ],
        out_specs=pl.BlockSpec((depth, 2 * block), lambda j: (0, j)),
        out_shape=jax.ShapeDtypeStruct((depth, count * 2 * block), BF),
        scratch_shapes=[pltpu.VMEM((depth, toks), BF)],
        cost_estimate=pl.CostEstimate(
            flops=4 * toks * depth * count * block,
            bytes_accessed=4 * depth * count * block + 2 * toks * depth,
            transcendentals=0,
        ),
        name="parts",
    )(tokens, slopes)


def backward(slopes, gate_weight, up_weight, gate_mask, up_mask, counts):
    block = gate_weight.shape[0] // gate_mask.shape[0]
    depth = gate_weight.shape[0]
    toks = slopes[0].shape[0]
    total = sum(counts)
    starts = [sum(counts[:i]) for i in range(len(counts))]

    def kernel(gm, um, *refs):
        gw, uw, out = refs[-3], refs[-2], refs[-1]
        j = pl.program_id(0)
        pair = masked_pair(gw, uw, gm, um, block, j)

        @pl.when(j == 0)
        def _():
            out[...] = jnp.zeros_like(out)

        for start, count, s in zip(starts, counts, refs[: len(counts)]):

            @pl.when((j >= start) & (j < start + count))
            def _(s=s):
                out[...] += lax.dot_general(
                    s[...], pair, (((1,), (1,)), ((), ())), preferred_element_type=F32
                )

    def piece(start, count):
        return pl.BlockSpec(
            (toks, 2 * block), lambda j: (0, jnp.minimum(jnp.maximum(j - start, 0), count - 1))
        )

    smem = pl.BlockSpec(memory_space=pltpu.SMEM)
    return pl.pallas_call(
        kernel,
        grid=(total,),
        in_specs=[smem, smem]
        + [piece(start, count) for start, count in zip(starts, counts)]
        + [
            pl.BlockSpec((depth, block), lambda j: (0, j)),
            pl.BlockSpec((depth, block), lambda j: (0, j)),
        ],
        out_specs=pl.BlockSpec((toks, depth), lambda j: (0, 0)),
        out_shape=jax.ShapeDtypeStruct((toks, depth), F32),
        cost_estimate=pl.CostEstimate(
            flops=4 * toks * depth * total * block,
            bytes_accessed=4 * depth * total * block + 4 * toks * depth,
            transcendentals=0,
        ),
        name="backward",
    )(gate_mask, up_mask, *slopes, gate_weight, up_weight)


def finish(sums, gate_mask, up_mask, block, counts):
    rows = sums[0].shape[0]
    blocks_down = gate_mask.shape[0]
    share = rows // blocks_down
    total = sum(counts)

    def kernel(gm, um, *refs):
        gate_out, up_out = refs[-2], refs[-1]
        at = 0
        for count, s in zip(counts, refs):
            for c in range(count):
                columns = pl.ds(at * block, block)
                for b in range(blocks_down):
                    part = pl.ds(b * share, share)
                    g = s[part, pl.ds(2 * c * block, block)].astype(F32)
                    u = s[part, pl.ds((2 * c + 1) * block, block)].astype(F32)
                    gate_out[b, :, columns] = (g * gm[b, at].astype(F32)).astype(BF)
                    up_out[b, :, columns] = (u * um[b, at].astype(F32)).astype(BF)
                at += 1

    smem = pl.BlockSpec(memory_space=pltpu.SMEM)
    vmem = pl.BlockSpec(memory_space=pltpu.VMEM)
    shape = jax.ShapeDtypeStruct((blocks_down, share, total * block), BF)
    return pl.pallas_call(
        kernel,
        in_specs=[smem, smem] + [vmem] * len(sums),
        out_specs=[vmem, vmem],
        out_shape=[shape, shape],
        name="finish",
    )(gate_mask, up_mask, *sums)


def body(tokens, gate_weight, up_weight, gate_mask, up_mask, slope):
    block = gate_weight.shape[0] // gate_mask.shape[0]
    total = gate_mask.shape[1]
    rows = lax.axis_size("row")
    replicas = lax.axis_size("dp")
    cols = lax.axis_size("col")
    counts = (FIRST_SHARE, total - FIRST_SHARE) if FIRST_SHARE else (total,)
    gathered = lax.all_gather(tokens, "col", axis=0, tiled=True)
    hidden = None
    all_slopes, sums = [], []
    first = 0
    for count in counts:
        partial = forward(gathered, gate_weight, up_weight, gate_mask, up_mask, first, count)
        received = lax.all_to_all(partial, "row", 0, 0, tiled=True)
        hidden, slopes = activate(received, slope, block, first, count, rows, hidden)
        slopes = lax.all_gather(slopes, "row", axis=0, tiled=True)
        parts = parts_of(gathered, slopes, block, replicas, count)
        sums.append(lax.psum_scatter(parts, "dp", scatter_dimension=0, tiled=True))
        all_slopes.append(slopes)
        first += count
    share = backward(all_slopes, gate_weight, up_weight, gate_mask, up_mask, counts)
    pieces = lax.all_to_all(share, "col", 0, 0, tiled=True)
    input_grad = jnp.sum(pieces.reshape((cols, -1) + pieces.shape[1:]), axis=0).astype(BF)
    gate_grad, up_grad = finish(sums, gate_mask, up_mask, block, counts)
    return hidden, input_grad, gate_grad, up_grad


def solution(mesh):
    return jax.shard_map(
        body,
        mesh=mesh,
        in_specs=(
            P(("dp", "col"), "row"),
            P("row", "col"),
            P("row", "col"),
            P("row", "col"),
            P("row", "col"),
            P(("dp", "row"), "col"),
        ),
        out_specs=(
            P(("dp", "row"), "col"),
            P(("dp", "col"), "row"),
            P("row", "dp", "col"),
            P("row", "dp", "col"),
        ),
        check_vma=False,
    )
```

time: 387 us -> 204 us (0.53)
  waiting for transfers between devices: 293 us -> 48.7 us
  blocking collectives: 36.8 us -> 98.8 us
  Pallas kernels: 0 us -> 31.3 us
  local copies, waits for them, and re-layouts: 17.5 us -> 0.75 us
  matrix products: 10.6 us -> 0 us
  other arithmetic: 7.47 us -> 0.67 us
    all_gather x1 -> x0, waiting for transfers between devices: 166 us -> none  [body(): everyone = lax.all_gather(slopes, ('dp', 'row'), axis=0, tiled=True)]
    reduce_scatter x1 -> x2, waiting for transfers between devices: 80.5 us -> 29.2 us  [body(): sums.append(lax.psum_scatter(parts, 'dp', scatter_dimension=0, tiled=True))]
    unnamed x4 -> x2, waiting for transfers between devices: 46.5 us -> 0.03 us
    all_gather x0 -> x2, blocking collectives: none -> 31.4 us  [body(): slopes = lax.all_gather(slopes, 'row', axis=0, tiled=True)]
    pallas_call x0 -> x8, Pallas kernels: none -> 31.3 us  [the longest x2 8.42 us: parts_of(): pl.pallas_call(kernel, grid=(count,), in_specs=[pl.BlockSpec((toks, depth...]
    all_to_all x0 -> x1, blocking collectives: none -> 29.5 us  [body(): pieces = lax.all_to_all(share, 'col', 0, 0, tiled=True)]
    all_to_all x1 -> x2, waiting for transfers between devices: 0.01 us -> 19.5 us  [body(): received = lax.all_to_all(partial, 'row', 0, 0, tiled=True)]
    unnamed x19 -> x6, local copies, waits for them, and re-layouts: 13.2 us -> 0.75 us
  transfers between devices with their start and end apart: 4 -> 4, of which waited for: 3 -> 3; matrix products, arithmetic and copies ran while one was open for 4% -> 0% of each run, Pallas kernels for 0% -> 9%
where the time goes in v1:
time: 204 us; the launch traced here: 203 us
  blocking collectives  98.8 us (48%)
  waiting for transfers between devices  48.7 us (24%)
  Pallas kernels  31.3 us (15%)
  between operations  14.1 us (7%)
  starting transfers between devices  9.17 us (4%)
    all_gather x1, blocking collectives, body(): gathered = lax.all_gather(tokens, 'col', axis=0, tiled=True)  37.9 us
    all_gather x2, blocking collectives, body(): slopes = lax.all_gather(slopes, 'row', axis=0, tiled=True)  31.4 us
    all_to_all x1, blocking collectives, body(): pieces = lax.all_to_all(share, 'col', 0, 0, tiled=True)  29.5 us
    reduce_scatter x2, waiting for transfers between devices, body(): sums.append(lax.psum_scatter(parts, 'dp', scatter_dimension=0, tiled=True))  29.2 us
    all_to_all x2, waiting for transfers between devices, body(): received = lax.all_to_all(partial, 'row', 0, 0, tiled=True)  19.5 us
    all_to_all x2, starting transfers between devices, body(): received = lax.all_to_all(partial, 'row', 0, 0, tiled=True)  9.08 us
    pallas_call x2, Pallas kernels, parts_of(): pl.pallas_call(kernel, grid=(count,), in_specs=[pl.BlockSpec((toks, depth...  8.42 us
    pallas_call x2, Pallas kernels, forward(): pl.pallas_call(kernel, grid=(count,), in_specs=[smem, smem, pl.BlockSpec(...  7.96 us
  transfers between devices with their start and end apart: 4, of which 3 were waited for; matrix products, arithmetic and copies ran while one was open for 0% of the time, Pallas kernels for 9%

profile of v1, /device:TPU:6, one launch (start us, length us, event | category | flops | bytes accessed | tf_op | source)
XLA Modules:
  0.0 203.4 jit_solution(14787234364234558282)
XLA Ops:
  7.2 37.9 %all_gather.9.t = bf16[256,1024]{1,0:T(8,128)(2,1)} all-gather(bf16[16,1024]{1,0:T(8,128)(2,1)} %param.6), channel_id=1, replica_groups=mesh['dp'=8,'row'=4,'col'=16] {'col'}, dimensions={0}, use_global_device_ids=true | all-gather | bytes 557056 | tf_op jit(solution)/shard_map/all_gather | solution.py:228
  45.1 4.3 %forward.3 = bf16[256,1024]{1,0:T(8,128)(2,1)} custom-call(s32[8,7]{1,0:T(8,128)} %gm.7, s32[8,7]{1,0:T(8,128)} %um.7, bf16[256,1024]{1,0:T(8,128)(2,1)} %all_gather.9.t, bf16[1024,896]{1,0:T(8,128)(2,1)} %refs_2_.1, bf16[1024,896]{1,0:T(8,128)(2,1)} %refs_3_.1), custom_call_target="tpu_custom_call" | custom-call | flops 536870912 | bytes 2621440 | tf_op jit(solution)/shard_map/forward/pallas_call | solution.py:33
  49.4 5.6 %all-to-all-start.1 = ((bf16[4,64,1024]{2,1,0:T(8,128)(2,1)}), bf16[4,64,1024]{2,1,0:T(8,128)(2,1)S(1)}, u32[]{:S(2)}, u32[]{:S(2)}) async-start(bf16[4,64,1024]{2,1,0:T(8,128)(2,1)} %bitcast.6), calls=%async_computation.1 | async-start | bytes 1048576 | tf_op jit(solution)/shard_map/all_to_all | solution.py:234
  55.0 3.7 %forward.2 = bf16[256,768]{1,0:T(8,128)(2,1)} custom-call(s32[8,7]{1,0:T(8,128)} %gm.7, s32[8,7]{1,0:T(8,128)} %um.7, bf16[256,1024]{1,0:T(8,128)(2,1)} %all_gather.9.t, bf16[1024,896]{1,0:T(8,128)(2,1)} %refs_2_.1, bf16[1024,896]{1,0:T(8,128)(2,1)} %refs_3_.1), custom_call_target="tpu_custom_call" | custom-call | flops 402653184 | bytes 2097152 | tf_op jit(solution)/shard_map/forward/pallas_call | solution.py:33
  58.6 11.4 %all-to-all-done.1 = bf16[4,64,1024]{2,1,0:T(8,128)(2,1)S(1)} async-done(((bf16[4,64,1024]{2,1,0:T(8,128)(2,1)}), bf16[4,64,1024]{2,1,0:T(8,128)(2,1)S(1)}, u32[]{:S(2)}, u32[]{:S(2)}) %all-to-all-start.1) | async-done | bytes 524320 | tf_op jit(solution)/shard_map/all_to_all | solution.py:234
  70.0 0.0 copy-start
  70.0 3.5 %all-to-all-start = ((bf16[4,64,768]{2,1,0:T(8,128)(2,1)}), bf16[4,64,768]{2,1,0:T(8,128)(2,1)S(1)}, u32[]{:S(2)}, u32[]{:S(2)}) async-start(bf16[4,64,768]{2,1,0:T(8,128)(2,1)} %bitcast.9), calls=%async_computation | async-start | bytes 786432 | tf_op jit(solution)/shard_map/all_to_all | solution.py:234
  73.5 0.0 reduce-scatter.5.cloned.1.call-start
  73.5 0.0 copy-done
  73.5 3.1 %activate.2 = (bf16[64,896]{1,0:T(8,128)(2,1)}, bf16[64,1024]{1,0:T(8,128)(2,1)}) custom-call(bf16[256,1024]{1,0:T(8,128)(2,1)} %bitcast.7, bf16[64,896]{1,0:T(8,128)(2,1)} %refs_1_.3), custom_call_target="tpu_custom_call" | custom-call | flops 983040 | bytes 786432 | tf_op jit(solution)/shard_map/activate/pallas_call | solution.py:81
  76.7 8.1 %all-to-all-done = bf16[4,64,768]{2,1,0:T(8,128)(2,1)S(1)} async-done(((bf16[4,64,768]{2,1,0:T(8,128)(2,1)}), bf16[4,64,768]{2,1,0:T(8,128)(2,1)S(1)}, u32[]{:S(2)}, u32[]{:S(2)}) %all-to-all-start) | async-done | bytes 393248 | tf_op jit(solution)/shard_map/all_to_all | solution.py:234
  84.8 0.0 copy-start.1
  84.8 0.7 copy-done.1
  85.5 2.5 %activate.3 = (bf16[64,896]{1,0:T(8,128)(2,1)}, bf16[64,768]{1,0:T(8,128)(2,1)}) custom-call(bf16[256,768]{1,0:T(8,128)(2,1)} %bitcast.8, bf16[64,896]{1,0:T(8,128)(2,1)} %refs_1_.3, bf16[64,896]{1,0:T(8,128)(2,1)} %get-tuple-element.10.refs_2_), custom_call_target="tpu_custom_call", output_to_operand_aliasing={{0}: (2, {})} | custom-call | flops 737280 | bytes 589824 | tf_op jit(solution)/shard_map/activate/pallas_call | solution.py:81
  88.0 16.0 %all_gather.11.refs_1_.s = bf16[256,768]{1,0:T(8,128)(2,1)} all-gather(bf16[64,768]{1,0:T(8,128)(2,1)} %get-tuple-element.13), channel_id=1, replica_groups=mesh['dp'=8,'row'=4,'col'=16] {'row'}, dimensions={0}, use_global_device_ids=true | all-gather | bytes 491520 | tf_op jit(solution)/shard_map/all_gather | solution.py:236
  104.0 0.0 copy-start.2
  104.0 3.9 %parts.3 = bf16[1024,768]{1,0:T(8,128)(2,1)} custom-call(bf16[256,1024]{1,0:T(8,128)(2,1)} %all_gather.9.t, bf16[256,768]{1,0:T(8,128)(2,1)} %all_gather.11.refs_1_.s), custom_call_target="tpu_custom_call" | custom-call | flops 402653184 | bytes 2097152 | tf_op jit(solution)/shard_map/parts/pallas_call | solution.py:120
  107.9 0.0 reduce-scatter.5.cloned.1.call-update
  107.9 0.0 reduce-scatter.3.cloned.1.call-start
  108.0 0.0 copy-done.2
  108.0 15.4 %all_gather.10.refs_0_.s = bf16[256,1024]{1,0:T(8,128)(2,1)} all-gather(bf16[64,1024]{1,0:T(8,128)(2,1)S(1)} %copy-done.2), channel_id=1, replica_groups=mesh['dp'=8,'row'=4,'col'=16] {'row'}, dimensions={0}, use_global_device_ids=true | all-gather | bytes 655360 | tf_op jit(solution)/shard_map/all_gather | solution.py:236
  123.4 4.5 %parts.2 = bf16[1024,1024]{1,0:T(8,128)(2,1)} custom-call(bf16[256,1024]{1,0:T(8,128)(2,1)} %all_gather.9.t, bf16[256,1024]{1,0:T(8,128)(2,1)} %all_gather.10.refs_0_.s), custom_call_target="tpu_custom_call" | custom-call | flops 536870912 | bytes 2621440 | tf_op jit(solution)/shard_map/parts/pallas_call | solution.py:120
  127.9 0.0 reduce-scatter.3.cloned.1.call-update
  128.0 7.4 %backward.1 = f32[256,1024]{1,0:T(8,128)} custom-call(s32[8,7]{1,0:T(8,128)} %gm.7, s32[8,7]{1,0:T(8,128)} %um.7, bf16[256,1024]{1,0:T(8,128)(2,1)} %all_gather.10.refs_0_.s, bf16[256,768]{1,0:T(8,128)(2,1)} %all_gather.11.refs_1_.s, bf16[1024,896]{1,0:T(8,128)(2,1)} %refs_2_.1, bf16[1024,896]{1,0:T(8,128)(2,1)} %refs_3_.1), custom_call_target="tpu_custom_call" | custom-call | flops 939524096 | bytes 4718592 | tf_op jit(solution)/shard_map/backward/pallas_call | solution.py:169
  135.3 29.5 %all_to_all.31 = f32[16,16,1024]{2,1,0:T(8,128)S(1)} all-to-all(f32[16,16,1024]{2,1,0:T(8,128)} %bitcast.5), channel_id=1, replica_groups=mesh['dp'=8,'row'=4,'col'=16] {'col'}, dimensions={0} | all-to-all | bytes 2097152 | tf_op jit(solution)/shard_map/all_to_all | solution.py:242
  164.8 0.7 reduce_sum.9
  165.5 0.0 reduce-scatter.5.cloned.1.call-done.refs_1_
  165.5 29.2 %reduce-scatter.3.cloned.1.call-done.refs_0_ = bf16[128,1024]{1,0:T(8,128)(2,1)} async-done(((bf16[1024,1024]{1,0:T(8,128)(2,1)}), bf16[128,1024]{1,0:T(8,128)(2,1)}) %reduce-scatter.3.cloned.1.call-update) | async-done | bytes 262160 | tf_op jit(solution)/shard_map/reduce_scatter | solution.py:238
  194.7 1.9 finish.1
Async XLA Ops:
  49.4 20.6 %all-to-all-start.1 = ((bf16[4,64,1024]{2,1,0:T(8,128)(2,1)}), bf16[4,64,1024]{2,1,0:T(8,128)(2,1)S(1)}, u32[]{:S(2)}, u32[]{:S(2)}) async-start(bf16[4,64,1024]{2,1,0:T(8,128)(2,1)} %bitcast.6), calls=%async_computation.1 | async-start | bytes 1048576 | tf_op jit(solution)/shard_map/all_to_all | solution.py:234
  70.0 3.5 %copy-start = (bf16[4,64,1024]{2,1,0:T(8,128)(2,1)}, bf16[4,64,1024]{2,1,0:T(8,128)(2,1)S(1)}, u32[]{:S(2)}) copy-start(bf16[4,64,1024]{2,1,0:T(8,128)(2,1)S(1)} %all-to-all-done.1) | copy-start | bytes 1572868
  70.0 14.8 %all-to-all-start = ((bf16[4,64,768]{2,1,0:T(8,128)(2,1)}), bf16[4,64,768]{2,1,0:T(8,128)(2,1)S(1)}, u32[]{:S(2)}, u32[]{:S(2)}) async-start(bf16[4,64,768]{2,1,0:T(8,128)(2,1)} %bitcast.9), calls=%async_computation | async-start | bytes 786432 | tf_op jit(solution)/shard_map/all_to_all | solution.py:234
  73.5 92.0 %reduce-scatter.5.cloned.1.call-start = ((), (), s32[]{:S(2)}) async-start(), calls=%async_computation.6 | async-start | bytes 1769472 | tf_op jit(solution)/shard_map/reduce_scatter | solution.py:238
  84.8 0.7 copy-start.1
  104.0 4.0 %copy-start.2 = (bf16[64,1024]{1,0:T(8,128)(2,1)S(1)}, bf16[64,1024]{1,0:T(8,128)(2,1)}, u32[]{:S(2)}) copy-start(bf16[64,1024]{1,0:T(8,128)(2,1)} %get-tuple-element.12) | copy-start | bytes 393220
  107.9 86.8 %reduce-scatter.3.cloned.1.call-start = ((), (), s32[]{:S(2)}) async-start(), calls=%async_computation.5 | async-start | bytes 2359296 | tf_op jit(solution)/shard_map/reduce_scatter | solution.py:238
Sparse Core Ops, SparseCore 0:
  108.1 39.4 reduce-scatter.4
  150.4 44.2 reduce-scatter.2
